TPU v7x, 256 devices: a whole 4x4x8 slice. The times are simulated.
256 devices in a mesh: front: 16 (over z, core), tile: 16 (over y, x).
Axes of the slice: x: 4, y: 4, z: 8, core: 2. Of those that a mesh axis runs over, the one named last changes fastest.
Arguments:
- pieces: bfloat16 [18432, 256, 128], P(('front', 'tile')), may hold values from -1.59375 to 1.59375
- dest_front: int32 [18432, 1], P(('front', 'tile')), may hold values from 0 to 15; in each aligned block of 72 rows (0 to 71, 72 to 143, ...) at most 9 rows name the same one
- dest_slot: int32 [18432], P(('front', 'tile')), may hold values from 0 to 3
- parent_u: bfloat16 [4096, 4096], P('front', 'tile'), may hold values from -1.59375 to 1.59375
- parent_v: bfloat16 [4096, 4096], P('front', 'tile'), may hold values from -1.59375 to 1.59375
- sketch: bfloat16 [256, 64], replicated, may hold values from -6 to 6
- pivot_inverse: bfloat16 [4096, 256], P('front'), may hold values from -0.01171875 to 0.01171875
Outputs:
- coeff: bfloat16 [4096, 4096], P('front', 'tile')
- cores: float32 [65536, 4096], P(('front', 'tile'))
Inputs may be any that keep to these rules, and one draw needn't show every extreme that they name: `dest_front`: among the 72 rows of one device at most 9 name any one front, a bound that some block reaches.
All inputs are finite; a program needn't handle non-finite values.
Results may differ from a plain program's by a relative error of at most 0.017.
Values may be sent and summed in bfloat16 or wider, within the bound.
No kernel may reach another device: no remote copies, remote signals or barrier semaphores. Data moves between devices by JAX's collectives and lax.ppermute only.
A program may use at most 128 MiB of HBM per device.

v0:
```python
import jax
import jax.numpy as jnp
from jax import lax
from jax.sharding import PartitionSpec as P

B = 256
R = 64
TILES_DEV = 4
CAP = 9


def sketch_pass(arrived, sketch):
    left_rows = arrived[..., :R]
    right_rows = arrived[..., R:]
    small = jnp.einsum(
        "...br,bk->...rk", right_rows, sketch, preferred_element_type=jnp.float32
    ).astype(jnp.bfloat16)
    return jnp.einsum("...br,...rk->...bk", left_rows, small, preferred_element_type=jnp.float32)


def orthonormal_basis(block_unit):
    gram_matrix = jnp.einsum(
        "naj,nav->njv", block_unit, block_unit, precision=lax.Precision.HIGHEST
    )
    lower = jnp.linalg.cholesky(gram_matrix)
    solved = jax.scipy.linalg.solve_triangular(lower, jnp.swapaxes(block_unit, 1, 2), lower=True)
    return jnp.swapaxes(solved, 1, 2)


def expand(factor, small):
    return jnp.einsum("pbr,prk->pbk", factor, small, preferred_element_type=jnp.float32)


def project(factor, other):
    return jnp.einsum("pbr,pbk->prk", factor, other, preferred_element_type=jnp.float32).astype(
        jnp.bfloat16
    )


def shards(pieces, dest_front, dest_slot, parent_u, parent_v, sketch, pivot_inverse):
    fronts = lax.axis_size("front")
    front_ids = dest_front[:, 0]
    front_marks = (front_ids[:, None] == jnp.arange(fronts, dtype=jnp.int32)[None, :]).astype(
        jnp.int32
    )
    prior_level = jnp.sum((jnp.cumsum(front_marks, axis=0) - front_marks) * front_marks, axis=1)
    places = front_ids * CAP + prior_level
    outgoing = (
        jnp.zeros((fronts * CAP, B, 2 * R), jnp.bfloat16)
        .at[places]
        .set(pieces)
        .reshape(fronts, CAP, B, 2 * R)
    )
    out_slots = (
        jnp.full((fronts * CAP,), TILES_DEV, jnp.int32)
        .at[places]
        .set(dest_slot)
        .reshape(fronts, CAP)
    )
    received, slot_ids = (
        lax.all_to_all(outgoing, "front", split_axis=0, concat_axis=0, tiled=True),
        lax.all_to_all(out_slots, "front", split_axis=0, concat_axis=0, tiled=True),
    )
    sketched = sketch_pass(received, sketch)
    slot_count = fronts * CAP
    piece_left = received[..., :R].reshape(slot_count, B, R)
    piece_right = received[..., R:].reshape(slot_count, B, R)
    sketched = sketched.reshape(slot_count, B, R)
    owner_mask = (
        slot_ids.reshape(slot_count)[None, :] == jnp.arange(TILES_DEV, dtype=jnp.int32)[:, None]
    )
    owner_float = owner_mask.astype(jnp.float32)
    owner_halves = owner_mask.astype(jnp.bfloat16)
    owned_left_rows = parent_u.reshape(B, TILES_DEV, R).transpose(1, 0, 2)
    own_right = parent_v.reshape(B, TILES_DEV, R).transpose(1, 0, 2)

    def collect(per_piece, parent_term):
        return (
            jnp.einsum("sp,pbk->sbk", owner_float, per_piece, precision=lax.Precision.HIGHEST)
            + parent_term
        )

    def select(field_values):
        return jnp.einsum(
            "eo,elj->olj", owner_halves, field_values, preferred_element_type=jnp.float32
        ).astype(jnp.bfloat16)

    y_start = collect(
        sketched, sketch_pass(jnp.concatenate((owned_left_rows, own_right), axis=2), sketch)
    )
    q_start = orthonormal_basis(y_start).astype(jnp.bfloat16)
    z_mid = collect(
        expand(piece_right, project(piece_left, select(q_start))),
        expand(own_right, project(owned_left_rows, q_start)),
    ).astype(jnp.bfloat16)
    y_end = collect(
        expand(piece_left, project(piece_right, select(z_mid))),
        expand(owned_left_rows, project(own_right, z_mid)),
    )
    q_end = orthonormal_basis(y_end).astype(jnp.bfloat16)
    w_end = collect(
        expand(piece_right, project(piece_left, select(q_end))),
        expand(own_right, project(owned_left_rows, q_end)),
    ).astype(jnp.bfloat16)
    coeff = w_end.transpose(1, 0, 2).reshape(B, TILES_DEV * R)
    pivoted = jnp.dot(pivot_inverse, coeff, preferred_element_type=jnp.float32).astype(jnp.bfloat16)
    cores = jnp.einsum(
        "bi,bj->ij",
        coeff,
        lax.all_gather(pivoted, "tile", axis=1, tiled=True),
        preferred_element_type=jnp.float32,
    )
    return (coeff, cores)


def solution(mesh):
    return jax.shard_map(
        shards,
        mesh=mesh,
        in_specs=(
            P(("front", "tile"), None, None),
            P(("front", "tile"), None),
            P(("front", "tile")),
            P("front", "tile"),
            P("front", "tile"),
            P(),
            P("front", None),
        ),
        out_specs=(P("front", "tile"), P(("front", "tile"), None)),
        check_vma=False,
    )
```

profile of v0, /device:TPU:2, one launch (start us, length us, event | category | flops | bytes accessed | tf_op | source)
XLA Modules:
  0.0 533.4 jit_solution(12885000864077269159)
XLA Ops:
  7.2 0.0 copy-start
  7.2 0.8 fusion.70
  8.0 0.1 reduce_window_sum.11
  8.1 0.8 select_reduce_fusion.2
  8.9 0.7 fusion.76
  9.6 0.9 scatter_custom_fusion
  10.5 0.7 all_to_all.9
  11.2 8.6 %all-to-all-start = ((s32[16,1,9]{2,1,0:T(1,128)}), s32[16,1,9]{2,1,0:T(1,128)S(1)}, u32[]{:S(2)}, u32[]{:S(2)}) async-start(s32[16,1,9]{2,1,0:T(1,128)} %bitcast.3), calls=%async_computation | async-start | bytes 16384 | tf_op jit(solution)/shard_map/all_to_all | solution.py:62
  19.8 6.0 %broadcast_in_dim.7 = bf16[144,256,128]{2,1,0:T(8,128)(2,1)} broadcast(bf16[]{:T(256)} %constant.46.clone.1), dimensions={} | broadcast | bytes 9437186 | tf_op jit(solution)/shard_map/broadcast_in_dim | solution.py:49
  25.8 14.6 %scatter_fusion = bf16[144,256,128]{2,1,0:T(8,128)(2,1)} fusion(bf16[144,256,128]{2,1,0:T(8,128)(2,1)} %broadcast_in_dim.7, s32[72]{0:T(128)S(1)} %fusion.76, bf16[72,256,128]{2,1,0:T(8,128)(2,1)} %param.10), kind=kCustom, calls=%fused_computation.1 | custom fusion | bytes 14156064 | tf_op jit(solution)/shard_map/scatter | solution.py:51
  40.3 12.7 %copy.125 = bf16[144,256,128]{1,2,0:T(8,128)(2,1)} copy(bf16[144,256,128]{2,1,0:T(8,128)(2,1)} %scatter_fusion) | data formatting | bytes 18874368 | tf_op jit(solution)/shard_map/scatter | solution.py:51
  53.0 0.0 all-to-all-done
  53.0 0.0 copy-start.2
  53.0 0.0 copy-start.3
  53.0 0.0 copy-start.1
  53.1 7.4 %all-to-all-start.1 = ((bf16[16,9,256,128]{2,3,1,0:T(8,128)(2,1)}), bf16[16,9,256,128]{2,3,1,0:T(8,128)(2,1)}, u32[]{:S(2)}, u32[]{:S(2)}) async-start(bf16[16,9,256,128]{2,3,1,0:T(8,128)(2,1)} %bitcast.111), calls=%async_computation.1 | async-start | bytes 18874368 | tf_op jit(solution)/shard_map/all_to_all | solution.py:61
  60.5 0.2 all-gather.2.cloned.1.call-start
  60.7 0.0 copy-done.2
  60.7 0.1 copy.128
  60.8 0.0 copy-done.3
  60.8 0.1 copy.129
  61.0 0.0 copy-done.1
  61.0 0.4 fusion.52
  61.4 0.5 broadcast.57
  61.9 0.7 reduce.7
  62.6 0.1 eq.34
  62.6 204.5 %all-to-all-done.1 = bf16[16,9,256,128]{2,3,1,0:T(8,128)(2,1)} async-done(((bf16[16,9,256,128]{2,3,1,0:T(8,128)(2,1)}), bf16[16,9,256,128]{2,3,1,0:T(8,128)(2,1)}, u32[]{:S(2)}, u32[]{:S(2)}) %all-to-all-start.1) | async-done | bytes 9437216 | tf_op jit(solution)/shard_map/all_to_all | solution.py:61
  267.1 10.2 %fusion.20 = f32[16,9,256,64]{2,3,1,0:T(8,128)} fusion(bf16[256,64]{0,1:T(8,128)(2,1)S(1)} %copy-done.1, bf16[16,9,256,128]{2,3,1,0:T(8,128)(2,1)} %all-to-all-done.1), kind=kOutput, calls=%fused_computation.25 | convolution fusion | flops 604569600 | bytes 18907136 | tf_op jit(solution)/shard_map/...br,...rk->...bk/dot_general | solution.py:18
  277.4 11.7 %bitcast_add_fusion.5 = (f32[4,256,64]{1,0,2:T(4,128)S(1)}, f32[4,256,64]{1,0,2:T(4,128)S(1)}) fusion(f32[4,64,256]{2,1,0:T(8,128)S(1)} %fusion.52, f32[144,256,64]{1,2,0:T(8,128)} %bitcast.112, s32[144]{0:T(256)S(1)} %eq.34), kind=kOutput, calls=%fused_computation.48 | convolution fusion | flops 113312320 | bytes 10224192 | tf_op jit(solution)/shard_map/sp,pbk->sbk/dot_general | solution.py:79
  289.0 0.4 fusion.60
  289.4 0.1 copy.134
  289.5 23.5 %custom-call.8 = f32[4,64,64]{2,1,0:T(8,128)S(1)} custom-call(f32[4,64,64]{2,1,0:T(8,128)S(1)} %fusion.65), custom_call_target="Cholesky" | custom-call | tf_op jit(solution)/shard_map/jit(cholesky)/cholesky | solution.py:25
  313.0 0.1 compare_reduce_fusion.1
  313.1 0.1 select_bitcast_fusion.1
  313.2 20.1 %custom-call.9 = f32[4,1,64,64]{2,3,1,0:T(8,128)S(1)} custom-call(f32[4,1,64,64]{3,2,1,0:T(8,128)S(1)} %select_bitcast_fusion.1), custom_call_target="InvertDiagBlocksLowerTriangular" | custom-call | tf_op jit(solution)/shard_map/jit(_solve_triangular)/vmap()/triangular_solve | solution.py:26
  333.3 0.4 convolution_convert_fusion.4
  333.8 0.3 fusion.53
  334.0 3.7 convolution_convert_fusion.2
  337.7 9.4 %fusion.89 = (bf16[16,9,256,64]{2,3,1,0:T(8,128)(2,1)}, bf16[16,9,256,64]{2,3,1,0:T(8,128)(2,1)}) fusion(bf16[16,9,256,128]{2,3,1,0:T(8,128)(2,1)} %all-to-all-done.1), kind=kLoop, calls=%fused_computation.86 | loop fusion | bytes 18874368 | tf_op jit(solution)/shard_map/slice | solution.py:66
  347.1 12.5 %fusion.18 = f32[144,256,64]{1,2,0:T(8,128)} fusion(bf16[144,256,64]{1,2,0:T(8,128)(2,1)} %bitcast.108, bf16[144,256,64]{1,2,0:T(8,128)(2,1)} %bitcast.105, bf16[144,256,64]{1,0,2:T(8,128)(2,1)} %convolution_convert_fusion.2), kind=kOutput, calls=%fused_computation.23 | convolution fusion | flops 604569600 | bytes 23592960 | tf_op jit(solution)/shard_map/pbr,prk->pbk/dot_general | solution.py:31
  359.6 11.8 %fusion.45 = bf16[4,256,64]{1,0,2:T(4,128)(2,1)S(1)} fusion(f32[144,256,64]{1,2,0:T(8,128)} %fusion.18, f32[4,64,256]{2,1,0:T(8,128)S(1)} %fusion.53, s32[144]{0:T(256)S(1)} %eq.34), kind=kOutput, calls=%fused_computation.34 | convolution fusion | flops 113377856 | bytes 9830976 | tf_op jit(solution)/shard_map/sp,pbk->sbk/dot_general | solution.py:79
  371.4 3.7 convolution_convert_fusion.1
  375.1 0.3 fusion.54
  375.4 12.5 %fusion.16 = f32[144,256,64]{1,2,0:T(8,128)} fusion(bf16[144,256,64]{1,2,0:T(8,128)(2,1)} %bitcast.106, bf16[144,256,64]{1,2,0:T(8,128)(2,1)} %bitcast.109, bf16[144,256,64]{1,0,2:T(8,128)(2,1)} %convolution_convert_fusion.1), kind=kOutput, calls=%fused_computation.21 | convolution fusion | flops 604569600 | bytes 23592960 | tf_op jit(solution)/shard_map/pbr,prk->pbk/dot_general | solution.py:31
  387.9 11.7 %bitcast_add_fusion.2 = (f32[4,256,64]{1,0,2:T(4,128)S(1)}, f32[4,256,64]{1,0,2:T(4,128)S(1)}) fusion(f32[4,64,256]{2,1,0:T(8,128)S(1)} %fusion.54, f32[144,256,64]{1,2,0:T(8,128)} %fusion.16, s32[144]{0:T(256)S(1)} %eq.34), kind=kOutput, calls=%fused_computation.46 | convolution fusion | flops 113312320 | bytes 10224192 | tf_op jit(solution)/shard_map/sp,pbk->sbk/dot_general | solution.py:79
  399.6 0.4 fusion.57
  399.9 0.1 copy.149
  400.1 23.5 %custom-call.10 = f32[4,64,64]{2,1,0:T(8,128)S(1)} custom-call(f32[4,64,64]{2,1,0:T(8,128)S(1)} %fusion.63), custom_call_target="Cholesky" | custom-call | tf_op jit(solution)/shard_map/jit(cholesky)/cholesky | solution.py:25
  423.6 0.1 compare_reduce_fusion
  423.7 0.1 select_bitcast_fusion
  423.8 19.9 %custom-call.11 = f32[4,1,64,64]{2,3,1,0:T(8,128)S(1)} custom-call(f32[4,1,64,64]{3,2,1,0:T(8,128)S(1)} %select_bitcast_fusion), custom_call_target="InvertDiagBlocksLowerTriangular" | custom-call | tf_op jit(solution)/shard_map/jit(_solve_triangular)/vmap()/triangular_solve | solution.py:26
  443.7 0.4 convolution_convert_fusion.3
  444.1 0.3 fusion.55
  444.4 3.7 convolution_convert_fusion
  448.0 12.5 %fusion.14 = f32[144,256,64]{1,2,0:T(8,128)} fusion(bf16[144,256,64]{1,2,0:T(8,128)(2,1)} %bitcast.110, bf16[144,256,64]{1,2,0:T(8,128)(2,1)} %bitcast.107, bf16[144,256,64]{1,0,2:T(8,128)(2,1)} %convolution_convert_fusion), kind=kOutput, calls=%fused_computation.19 | convolution fusion | flops 604569600 | bytes 23592960 | tf_op jit(solution)/shard_map/pbr,prk->pbk/dot_general | solution.py:31
  460.5 11.7 %fusion.48 = bf16[256,4,64]{0,1,2:T(4,128)(2,1)S(1)} fusion(f32[144,256,64]{1,2,0:T(8,128)} %fusion.14, f32[4,64,256]{2,1,0:T(8,128)S(1)} %fusion.55, s32[144]{0:T(256)S(1)} %eq.34), kind=kOutput, calls=%fused_computation.35 | convolution fusion | flops 113377856 | bytes 9830976 | tf_op jit(solution)/shard_map/sp,pbk->sbk/dot_general | solution.py:79
  472.2 0.0 copy-done
  472.2 0.9 fusion.51
  473.1 0.0 all-gather.2.cloned.1.call-update
  473.2 0.8 copy.158
  473.9 48.0 %all-gather.2.cloned.1.call-done = bf16[256,4096]{0,1:T(8,128)(2,1)} async-done(((bf16[256,256]{0,1:T(8,128)(2,1)}), bf16[256,4096]{0,1:T(8,128)(2,1)}) %all-gather.2.cloned.1.call-update) | async-done | bytes 2097168 | tf_op jit(solution)/shard_map/all_gather | solution.py:110
  521.9 4.3 fusion.90
  (7 shorter events, 0.1 us)
Async XLA Ops:
  7.2 465.1 %copy-start = (bf16[256,256]{1,0:T(8,128)(2,1)S(1)}, bf16[256,256]{1,0:T(8,128)(2,1)}, u32[]{:S(2)}) copy-start(bf16[256,256]{1,0:T(8,128)(2,1)} %param.16) | copy-start | bytes 393220
  11.2 41.8 %all-to-all-start = ((s32[16,1,9]{2,1,0:T(1,128)}), s32[16,1,9]{2,1,0:T(1,128)S(1)}, u32[]{:S(2)}, u32[]{:S(2)}) async-start(s32[16,1,9]{2,1,0:T(1,128)} %bitcast.3), calls=%async_computation | async-start | bytes 16384 | tf_op jit(solution)/shard_map/all_to_all | solution.py:62
  53.0 7.7 %copy-start.2 = (bf16[256,256]{1,0:T(8,128)(2,1)S(1)}, bf16[256,256]{1,0:T(8,128)(2,1)}, u32[]{:S(2)}) copy-start(bf16[256,256]{1,0:T(8,128)(2,1)} %param.14) | copy-start | bytes 393220
  53.0 7.8 %copy-start.3 = (bf16[256,256]{1,0:T(8,128)(2,1)S(1)}, bf16[256,256]{1,0:T(8,128)(2,1)}, u32[]{:S(2)}) copy-start(bf16[256,256]{1,0:T(8,128)(2,1)} %param.13) | copy-start | bytes 393220
  53.0 7.9 %copy-start.1 = (bf16[256,64]{0,1:T(8,128)(2,1)S(1)}, bf16[256,64]{0,1:T(8,128)(2,1)}, u32[]{:S(2)}) copy-start(bf16[256,64]{0,1:T(8,128)(2,1)} %param.15) | copy-start | bytes 98308
  53.1 214.1 %all-to-all-start.1 = ((bf16[16,9,256,128]{2,3,1,0:T(8,128)(2,1)}), bf16[16,9,256,128]{2,3,1,0:T(8,128)(2,1)}, u32[]{:S(2)}, u32[]{:S(2)}) async-start(bf16[16,9,256,128]{2,3,1,0:T(8,128)(2,1)} %bitcast.111), calls=%async_computation.1 | async-start | bytes 18874368 | tf_op jit(solution)/shard_map/all_to_all | solution.py:61
  60.5 461.5 %all-gather.2.cloned.1.call-start = ((), (), s32[]{:S(2)}) async-start(), calls=%async_computation.2 | async-start | bytes 2228224 | tf_op jit(solution)/shard_map/all_gather | solution.py:110
Sparse Core Ops, SparseCore 0:
  473.3 48.6 all-gather.1
where the time goes:
time: 537 us; the launch traced here: 533 us
  waiting for transfers between devices  253 us (47%)
  matrix products  114 us (21%)
  other arithmetic  90.4 us (17%)
  local copies, waits for them, and re-layouts  46.1 us (9%)
  starting transfers between devices  16.2 us (3%)
  between operations  14.5 us (3%)
    all_to_all x1, waiting for transfers between devices, shards(): lax.all_to_all(outgoing, 'front', split_axis=0, concat_axis=0, tiled=True)  204 us
    all_gather x1, waiting for transfers between devices, shards(): lax.all_gather(pivoted, 'tile', axis=1, tiled=True)  48 us
    another operation x7, other arithmetic, orthonormal_basis(): lower = jnp.linalg.cholesky(gram_matrix)  47.2 us
    dot_general x4, matrix products, collect(): jnp.einsum('sp,pbk->sbk', owner_float, per_piece, precision=lax.Precision...  46.8 us
    another operation x5, other arithmetic, orthonormal_basis(): jax.scipy.linalg.solve_triangular(lower, jnp.swapaxes(block_unit, 1, 2),...  40.1 us
    dot_general x6, matrix products, expand(): jnp.einsum('pbr,prk->pbk', factor, small, preferred_element_type=jnp.floa...  38.4 us
    scatter x2, local copies, waits for them, and re-layouts, shards(): outgoing = jnp.zeros((fronts * CAP, B, 2 * R), jnp.bfloat16).at[places].s...  27.3 us
    dot_general x3, matrix products, select(): jnp.einsum('eo,elj->olj', owner_halves, field_values, preferred_element_t...  11 us
  transfers between devices with their start and end apart: 3, of which 2 were waited for; matrix products, arithmetic and copies ran while one was open for 7% of the time, Pallas kernels for 0%

commit v1 on v0

--- a/solution.py
+++ b/solution.py
@@ -7,6 +7,13 @@
 R = 64
 TILES_DEV = 4
 CAP = 9
+
+
+def samples_all_balance(xin, peer_axis, dim_no=1):
+    inter = lax.axis_size(peer_axis)
+    z_new = jnp.stack([xin] * inter, axis=0)
+    local_part = lax.all_to_all(z_new, peer_axis, 0, 0)
+    return jnp.concatenate(local_part, axis=dim_no)
 
 
 def sketch_pass(arrived, sketch):
@@ -105,10 +112,7 @@
     coeff = w_end.transpose(1, 0, 2).reshape(B, TILES_DEV * R)
     pivoted = jnp.dot(pivot_inverse, coeff, preferred_element_type=jnp.float32).astype(jnp.bfloat16)
     cores = jnp.einsum(
-        "bi,bj->ij",
-        coeff,
-        lax.all_gather(pivoted, "tile", axis=1, tiled=True),
-        preferred_element_type=jnp.float32,
+        "bi,bj->ij", coeff, samples_all_balance(pivoted, "tile"), preferred_element_type=jnp.float32
     )
     return (coeff, cores)
 

time: 537 us -> 514 us (0.957)
  waiting for transfers between devices: 253 us -> 231 us
  between operations: 14.5 us -> 1.17 us
  starting transfers between devices: 16.2 us -> 23.6 us
    all_gather x1 -> x0, waiting for transfers between devices: 48 us -> none  [shards(): lax.all_gather(pivoted, 'tile', axis=1, tiled=True)]
    all_to_all x0 -> x1, waiting for transfers between devices: none -> 26.1 us  [samples_all_balance(): local_part = lax.all_to_all(z_new, peer_axis, 0, 0)]
    all_to_all x0 -> x1, starting transfers between devices: none -> 7.38 us  [samples_all_balance(): local_part = lax.all_to_all(z_new, peer_axis, 0, 0)]
where the time goes in v1:
time: 514 us; the launch traced here: 505 us
  waiting for transfers between devices  231 us (45%)
  matrix products  112 us (22%)
  other arithmetic  90.2 us (18%)
  local copies, waits for them, and re-layouts  47.5 us (9%)
  starting transfers between devices  23.6 us (5%)
    all_to_all x1, waiting for transfers between devices, shards(): lax.all_to_all(outgoing, 'front', split_axis=0, concat_axis=0, tiled=True)  205 us
    dot_general x4, matrix products, collect(): jnp.einsum('sp,pbk->sbk', owner_float, per_piece, precision=lax.Precision...  47.3 us
    another operation x7, other arithmetic, orthonormal_basis(): lower = jnp.linalg.cholesky(gram_matrix)  47.2 us
    another operation x5, other arithmetic, orthonormal_basis(): jax.scipy.linalg.solve_triangular(lower, jnp.swapaxes(block_unit, 1, 2),...  39.9 us
    dot_general x6, matrix products, expand(): jnp.einsum('pbr,prk->pbk', factor, small, preferred_element_type=jnp.floa...  38.4 us
    scatter x2, local copies, waits for them, and re-layouts, shards(): outgoing = jnp.zeros((fronts * CAP, B, 2 * R), jnp.bfloat16).at[places].s...  27.2 us
    all_to_all x1, waiting for transfers between devices, samples_all_balance(): local_part = lax.all_to_all(z_new, peer_axis, 0, 0)  26.1 us
    dot_general x3, matrix products, select(): jnp.einsum('eo,elj->olj', owner_halves, field_values, preferred_element_t...  11 us
  transfers between devices with their start and end apart: 3, of which 2 were waited for; matrix products, arithmetic and copies ran while one was open for 7% of the time, Pallas kernels for 0%

profile of v1, /device:TPU:2, one launch (start us, length us, event | category | flops | bytes accessed | tf_op | source)
XLA Modules:
  0.0 505.2 jit_solution(9617506911736732999)
XLA Ops:
  0.6 0.0 copy-start
  0.6 0.8 fusion.70
  1.4 0.1 reduce_window_sum.11
  1.5 0.8 select_reduce_fusion.2
  2.4 0.7 fusion.76
  3.0 0.9 scatter_custom_fusion
  4.0 0.7 all_to_all.12
  4.7 8.6 %all-to-all-start = ((s32[16,1,9]{2,1,0:T(1,128)}), s32[16,1,9]{2,1,0:T(1,128)S(1)}, u32[]{:S(2)}, u32[]{:S(2)}) async-start(s32[16,1,9]{2,1,0:T(1,128)} %bitcast.3), calls=%async_computation | async-start | bytes 16384 | tf_op jit(solution)/shard_map/all_to_all | solution.py:69
  13.2 6.0 %broadcast_in_dim.7 = bf16[144,256,128]{2,1,0:T(8,128)(2,1)} broadcast(bf16[]{:T(256)} %constant.46.clone.1), dimensions={} | broadcast | bytes 9437186 | tf_op jit(solution)/shard_map/broadcast_in_dim | solution.py:56
  19.2 14.5 %scatter_fusion = bf16[144,256,128]{2,1,0:T(8,128)(2,1)} fusion(bf16[144,256,128]{2,1,0:T(8,128)(2,1)} %broadcast_in_dim.7, s32[72]{0:T(128)S(1)} %fusion.76, bf16[72,256,128]{2,1,0:T(8,128)(2,1)} %param.10), kind=kCustom, calls=%fused_computation.1 | custom fusion | bytes 14156064 | tf_op jit(solution)/shard_map/scatter | solution.py:58
  33.7 12.7 %copy.126 = bf16[144,256,128]{1,2,0:T(8,128)(2,1)} copy(bf16[144,256,128]{2,1,0:T(8,128)(2,1)} %scatter_fusion) | data formatting | bytes 18874368 | tf_op jit(solution)/shard_map/scatter | solution.py:58
  46.5 0.0 all-to-all-done
  46.5 0.0 copy-start.2
  46.5 0.0 copy-start.3
  46.5 0.0 copy-start.1
  46.5 7.7 %all-to-all-start.1 = ((bf16[16,9,256,128]{2,3,1,0:T(8,128)(2,1)}), bf16[16,9,256,128]{2,3,1,0:T(8,128)(2,1)}, u32[]{:S(2)}, u32[]{:S(2)}) async-start(bf16[16,9,256,128]{2,3,1,0:T(8,128)(2,1)} %bitcast.114), calls=%async_computation.1 | async-start | bytes 18874368 | tf_op jit(solution)/shard_map/all_to_all | solution.py:68
  54.2 0.0 copy-done.2
  54.2 0.1 copy.129
  54.3 0.0 copy-done.3
  54.3 0.1 copy.130
  54.4 0.0 copy-done.1
  54.4 0.4 fusion.52
  54.8 0.5 broadcast.59
  55.3 0.7 reduce.7
  56.0 0.1 eq.34
  56.1 204.7 %all-to-all-done.1 = bf16[16,9,256,128]{2,3,1,0:T(8,128)(2,1)} async-done(((bf16[16,9,256,128]{2,3,1,0:T(8,128)(2,1)}), bf16[16,9,256,128]{2,3,1,0:T(8,128)(2,1)}, u32[]{:S(2)}, u32[]{:S(2)}) %all-to-all-start.1) | async-done | bytes 9437216 | tf_op jit(solution)/shard_map/all_to_all | solution.py:68
  260.8 10.2 %fusion.20 = f32[16,9,256,64]{2,3,1,0:T(8,128)} fusion(bf16[256,64]{0,1:T(8,128)(2,1)S(1)} %copy-done.1, bf16[16,9,256,128]{2,3,1,0:T(8,128)(2,1)} %all-to-all-done.1), kind=kOutput, calls=%fused_computation.25 | convolution fusion | flops 604569600 | bytes 18907136 | tf_op jit(solution)/shard_map/...br,...rk->...bk/dot_general | solution.py:25
  271.0 11.7 %bitcast_add_fusion.5 = (f32[4,256,64]{1,0,2:T(4,128)S(1)}, f32[4,256,64]{1,0,2:T(4,128)S(1)}) fusion(f32[4,64,256]{2,1,0:T(8,128)S(1)} %fusion.52, f32[144,256,64]{1,2,0:T(8,128)} %bitcast.115, s32[144]{0:T(256)S(1)} %eq.34), kind=kOutput, calls=%fused_computation.48 | convolution fusion | flops 113312320 | bytes 10224192 | tf_op jit(solution)/shard_map/sp,pbk->sbk/dot_general | solution.py:86
  282.7 0.4 fusion.60
  283.1 0.1 copy.135
  283.2 23.5 %custom-call.8 = f32[4,64,64]{2,1,0:T(8,128)S(1)} custom-call(f32[4,64,64]{2,1,0:T(8,128)S(1)} %fusion.65), custom_call_target="Cholesky" | custom-call | tf_op jit(solution)/shard_map/jit(cholesky)/cholesky | solution.py:32
  306.7 0.1 compare_reduce_fusion.1
  306.8 0.1 select_bitcast_fusion.1
  306.9 20.1 %custom-call.9 = f32[4,1,64,64]{2,3,1,0:T(8,128)S(1)} custom-call(f32[4,1,64,64]{3,2,1,0:T(8,128)S(1)} %select_bitcast_fusion.1), custom_call_target="InvertDiagBlocksLowerTriangular" | custom-call | tf_op jit(solution)/shard_map/jit(_solve_triangular)/vmap()/triangular_solve | solution.py:33
  327.0 0.4 convolution_convert_fusion.4
  327.4 0.3 fusion.53
  327.7 3.7 convolution_convert_fusion.2
  331.3 9.4 %fusion.89 = (bf16[16,9,256,64]{2,3,1,0:T(8,128)(2,1)}, bf16[16,9,256,64]{2,3,1,0:T(8,128)(2,1)}) fusion(bf16[16,9,256,128]{2,3,1,0:T(8,128)(2,1)} %all-to-all-done.1), kind=kLoop, calls=%fused_computation.86 | loop fusion | bytes 18874368 | tf_op jit(solution)/shard_map/slice | solution.py:73
  340.7 12.5 %fusion.18 = f32[144,256,64]{1,2,0:T(8,128)} fusion(bf16[144,256,64]{1,2,0:T(8,128)(2,1)} %bitcast.111, bf16[144,256,64]{1,2,0:T(8,128)(2,1)} %bitcast.108, bf16[144,256,64]{1,0,2:T(8,128)(2,1)} %convolution_convert_fusion.2), kind=kOutput, calls=%fused_computation.23 | convolution fusion | flops 604569600 | bytes 23592960 | tf_op jit(solution)/shard_map/pbr,prk->pbk/dot_general | solution.py:38
  353.3 11.8 %fusion.45 = bf16[4,256,64]{1,0,2:T(4,128)(2,1)S(1)} fusion(f32[144,256,64]{1,2,0:T(8,128)} %fusion.18, f32[4,64,256]{2,1,0:T(8,128)S(1)} %fusion.53, s32[144]{0:T(256)S(1)} %eq.34), kind=kOutput, calls=%fused_computation.34 | convolution fusion | flops 113377856 | bytes 9830976 | tf_op jit(solution)/shard_map/sp,pbk->sbk/dot_general | solution.py:86
  365.1 3.7 convolution_convert_fusion.1
  368.7 0.3 fusion.54
  369.0 12.5 %fusion.16 = f32[144,256,64]{1,2,0:T(8,128)} fusion(bf16[144,256,64]{1,2,0:T(8,128)(2,1)} %bitcast.109, bf16[144,256,64]{1,2,0:T(8,128)(2,1)} %bitcast.112, bf16[144,256,64]{1,0,2:T(8,128)(2,1)} %convolution_convert_fusion.1), kind=kOutput, calls=%fused_computation.21 | convolution fusion | flops 604569600 | bytes 23592960 | tf_op jit(solution)/shard_map/pbr,prk->pbk/dot_general | solution.py:38
  381.6 11.9 %bitcast_add_fusion.2 = (f32[4,256,64]{1,0,2:T(4,128)S(1)}, f32[4,256,64]{1,0,2:T(4,128)S(1)}) fusion(f32[4,64,256]{2,1,0:T(8,128)S(1)} %fusion.54, f32[144,256,64]{1,2,0:T(8,128)} %fusion.16, s32[144]{0:T(256)S(1)} %eq.34), kind=kOutput, calls=%fused_computation.46 | convolution fusion | flops 113312320 | bytes 10224192 | tf_op jit(solution)/shard_map/sp,pbk->sbk/dot_general | solution.py:86
  393.4 0.4 fusion.57
  393.8 0.1 copy.150
  393.9 23.5 %custom-call.10 = f32[4,64,64]{2,1,0:T(8,128)S(1)} custom-call(f32[4,64,64]{2,1,0:T(8,128)S(1)} %fusion.63), custom_call_target="Cholesky" | custom-call | tf_op jit(solution)/shard_map/jit(cholesky)/cholesky | solution.py:32
  417.4 0.1 compare_reduce_fusion
  417.6 0.1 select_bitcast_fusion
  417.6 19.7 %custom-call.11 = f32[4,1,64,64]{2,3,1,0:T(8,128)S(1)} custom-call(f32[4,1,64,64]{3,2,1,0:T(8,128)S(1)} %select_bitcast_fusion), custom_call_target="InvertDiagBlocksLowerTriangular" | custom-call | tf_op jit(solution)/shard_map/jit(_solve_triangular)/vmap()/triangular_solve | solution.py:33
  437.3 0.4 convolution_convert_fusion.3
  437.8 0.3 fusion.55
  438.1 3.7 convolution_convert_fusion
  441.7 12.5 %fusion.14 = f32[144,256,64]{1,2,0:T(8,128)} fusion(bf16[144,256,64]{1,2,0:T(8,128)(2,1)} %bitcast.113, bf16[144,256,64]{1,2,0:T(8,128)(2,1)} %bitcast.110, bf16[144,256,64]{1,0,2:T(8,128)(2,1)} %convolution_convert_fusion), kind=kOutput, calls=%fused_computation.19 | convolution fusion | flops 604569600 | bytes 23592960 | tf_op jit(solution)/shard_map/pbr,prk->pbk/dot_general | solution.py:38
  454.2 11.9 %fusion.48 = bf16[256,4,64]{0,1,2:T(4,128)(2,1)S(1)} fusion(f32[144,256,64]{1,2,0:T(8,128)} %fusion.14, f32[4,64,256]{2,1,0:T(8,128)S(1)} %fusion.55, s32[144]{0:T(256)S(1)} %eq.34), kind=kOutput, calls=%fused_computation.35 | convolution fusion | flops 113377856 | bytes 9830976 | tf_op jit(solution)/shard_map/sp,pbk->sbk/dot_general | solution.py:86
  466.2 0.0 copy-done
  466.2 0.2 fusion.51
  466.4 1.5 stack.2
  467.9 7.4 %all-to-all-start.2 = ((bf16[16,256,256]{1,2,0:T(8,128)(2,1)}), bf16[16,256,256]{1,2,0:T(8,128)(2,1)S(1)}, u32[]{:S(2)}, u32[]{:S(2)}) async-start(bf16[16,256,256]{1,2,0:T(8,128)(2,1)} %stack.2), calls=%async_computation.2 | async-start | bytes 4194304 | tf_op jit(solution)/shard_map/all_to_all | solution.py:15
  475.3 0.8 copy.159
  476.1 26.1 %all-to-all-done.2 = bf16[16,256,256]{1,2,0:T(8,128)(2,1)S(1)} async-done(((bf16[16,256,256]{1,2,0:T(8,128)(2,1)}), bf16[16,256,256]{1,2,0:T(8,128)(2,1)S(1)}, u32[]{:S(2)}, u32[]{:S(2)}) %all-to-all-start.2) | async-done | bytes 2097184 | tf_op jit(solution)/shard_map/all_to_all | solution.py:15
  502.1 2.8 fusion.90
  (7 shorter events, 0.1 us)
Async XLA Ops:
  0.6 465.5 %copy-start = (bf16[256,256]{1,0:T(8,128)(2,1)S(1)}, bf16[256,256]{1,0:T(8,128)(2,1)}, u32[]{:S(2)}) copy-start(bf16[256,256]{1,0:T(8,128)(2,1)} %param.16) | copy-start | bytes 393220
  4.7 41.8 %all-to-all-start = ((s32[16,1,9]{2,1,0:T(1,128)}), s32[16,1,9]{2,1,0:T(1,128)S(1)}, u32[]{:S(2)}, u32[]{:S(2)}) async-start(s32[16,1,9]{2,1,0:T(1,128)} %bitcast.3), calls=%async_computation | async-start | bytes 16384 | tf_op jit(solution)/shard_map/all_to_all | solution.py:69
  46.5 7.7 %copy-start.2 = (bf16[256,256]{1,0:T(8,128)(2,1)S(1)}, bf16[256,256]{1,0:T(8,128)(2,1)}, u32[]{:S(2)}) copy-start(bf16[256,256]{1,0:T(8,128)(2,1)} %param.14) | copy-start | bytes 393220
  46.5 7.8 %copy-start.3 = (bf16[256,256]{1,0:T(8,128)(2,1)S(1)}, bf16[256,256]{1,0:T(8,128)(2,1)}, u32[]{:S(2)}) copy-start(bf16[256,256]{1,0:T(8,128)(2,1)} %param.13) | copy-start | bytes 393220
  46.5 8.0 %copy-start.1 = (bf16[256,64]{0,1:T(8,128)(2,1)S(1)}, bf16[256,64]{0,1:T(8,128)(2,1)}, u32[]{:S(2)}) copy-start(bf16[256,64]{0,1:T(8,128)(2,1)} %param.15) | copy-start | bytes 98308
  46.5 214.3 %all-to-all-start.1 = ((bf16[16,9,256,128]{2,3,1,0:T(8,128)(2,1)}), bf16[16,9,256,128]{2,3,1,0:T(8,128)(2,1)}, u32[]{:S(2)}, u32[]{:S(2)}) async-start(bf16[16,9,256,128]{2,3,1,0:T(8,128)(2,1)} %bitcast.114), calls=%async_computation.1 | async-start | bytes 18874368 | tf_op jit(solution)/shard_map/all_to_all | solution.py:68
  467.9 34.2 %all-to-all-start.2 = ((bf16[16,256,256]{1,2,0:T(8,128)(2,1)}), bf16[16,256,256]{1,2,0:T(8,128)(2,1)S(1)}, u32[]{:S(2)}, u32[]{:S(2)}) async-start(bf16[16,256,256]{1,2,0:T(8,128)(2,1)} %stack.2), calls=%async_computation.2 | async-start | bytes 4194304 | tf_op jit(solution)/shard_map/all_to_all | solution.py:15
